TPU v7x, 32 devices: a whole 2x2x4 slice. The times are simulated.
32 devices in a mesh: pairs: 2 (over y), rows: 8 (over z, x), cols: 2 (over core).
Axes of the slice: x: 2, y: 2, z: 4, core: 2. Of those that a mesh axis runs over, the one named last changes fastest.
Arguments:
- left_image: bfloat16 [32, 1024, 128], P(('pairs', 'rows'), 'cols'), parts along dimension 0, may hold values from -6 to 6
- right_image: bfloat16 [32, 1024, 128], P(('pairs', 'rows'), 'cols'), parts along dimension 0, may hold values from -6 to 6
- weight: bfloat16 [1152, 256], replicated, may hold values from -0.1875 to 0.1875
- level_zero: bfloat16 [32, 1024, 256], P(('pairs', 'rows'), 'cols'), parts along dimension 0, may hold values from -6 to 6
- level_one: bfloat16 [32, 1024, 128], P(('pairs', 'rows'), 'cols'), parts along dimension 0, may hold values from -6 to 6
- level_two: bfloat16 [32, 1024, 64], P(('pairs', 'rows'), 'cols'), parts along dimension 0, may hold values from -6 to 6
- level_three: bfloat16 [32, 1024, 32], P(('pairs', 'rows'), 'cols'), parts along dimension 0, may hold values from -6 to 6
Outputs:
- grad_left_in: bfloat16 [32, 1024, 128], P(('pairs', 'rows'), 'cols'), parts along dimension 0
- grad_right_in: bfloat16 [32, 1024, 128], P(('pairs', 'rows'), 'cols'), parts along dimension 0
- weight_grad: float32 [512, 1152], P(('pairs', 'rows')), parts along dimension 0
There are 2 independent parts, one for each index of `pairs`. A program takes and returns all parts, laid end to end along the dimension named above; an argument that names none is the same for every part. Nothing has to cross between parts.
All inputs are finite; a program needn't handle non-finite values.
Results may differ from a plain program's by a relative error of at most 0.008.
Values may be sent and summed in bfloat16 or wider, within the bound.
A program may use at most 64 MiB of HBM per device.

v0:
```python
import functools
import math

import jax
import jax.numpy as jnp
from jax import lax
from jax.experimental import pallas as pl
from jax.experimental.pallas import tpu as pltpu
from jax.sharding import PartitionSpec as P

F32 = jnp.float32
BF16 = jnp.bfloat16
TILE = 16


def remote(src, dst, send, recv, row, col):
    return pltpu.make_async_remote_copy(
        src_ref=src,
        dst_ref=dst,
        send_sem=send,
        recv_sem=recv,
        device_id={"rows": row, "cols": col},
        device_id_type=pl.DeviceIdType.MESH,
    )


def matmul(a, b, dims):
    return lax.dot_general(a, b, (dims, ((), ())), preferred_element_type=F32)


def expansion(levels, reach, factor):
    source = lax.broadcasted_iota(jnp.int32, (levels, reach), 0)
    target = (reach - 1) - lax.broadcasted_iota(jnp.int32, (levels, reach), 1)
    bits = factor.bit_length() - 1
    hit = lax.shift_right_logical(target, jnp.int32(bits)) == source
    return jnp.where(hit, 1.0 / factor, 0.0).astype(BF16)


def kernel(
    rows, cols, left, right, weight_hbm, l0_hbm, l1_hbm, l2_hbm, l3_hbm, gl_out, gr_out, wg_out,
    weight, l0, l1, l2, l3, halo_row, halo_col, band_m, patch, left_feat, right_ext, ret_out, ret_in,
    grad, grad_edge, zed, part_out, part_in, acc, early, pair_out, pair_in, chunk, landed, whole,
    row_send, row_recv, col_send, col_recv, ext_send, ext_recv, ret_send, ret_recv,
    edge_send, edge_recv, part_send, part_recv, pair_send, pair_recv, chunk_send, chunk_recv, whole_send, whole_recv, load_sem,
):
    depth, band, cin = left.shape
    features = weight.shape[1]
    reach = l0.shape[2]
    blocks = band // reach
    quota = features // (rows * cols)
    r = lax.axis_index("rows")
    c = lax.axis_index("cols")
    other = 1 - c
    images = (left, right)
    group = rows * cols
    me = r * cols + c

    barrier = pltpu.get_barrier_semaphore()

    def greet(i, carry):
        peer = lax.rem(me + i, group)
        pl.semaphore_signal(
            barrier,
            inc=1,
            device_id={"rows": peer // cols, "cols": lax.rem(peer, cols)},
            device_id_type=pl.DeviceIdType.MESH,
        )
        return carry

    lax.fori_loop(1, group, greet, 0)
    loads = [
        pltpu.make_async_copy(src, dst, load_sem.at[k])
        for k, (src, dst) in enumerate(
            ((l0_hbm, l0), (l1_hbm, l1), (l2_hbm, l2), (l3_hbm, l3), (weight_hbm, weight))
        )
    ]
    for load in loads:
        load.start()
    pl.semaphore_wait(barrier, group - 1)

    near = pl.multiple_of(other * (band - TILE), TILE)

    def down(i):
        return remote(images[i].at[depth - 1], halo_row.at[0, i], row_send.at[0, i], row_recv.at[0, i], r + 1, c)

    def up(i):
        return remote(images[i].at[0], halo_row.at[1, i], row_send.at[1, i], row_recv.at[1, i], r - 1, c)

    def tile_mid(i):
        return remote(
            images[i].at[:, pl.ds(near, TILE)], halo_col.at[i, pl.ds(1, depth)],
            col_send.at[0, i], col_recv.at[0, i], r, other,
        )

    def tile_down(i):
        return remote(
            images[i].at[depth - 1, pl.ds(near, TILE)], halo_col.at[i, 0],
            col_send.at[1, i], col_recv.at[1, i], r + 1, other,
        )

    def tile_up(i):
        return remote(
            images[i].at[0, pl.ds(near, TILE)], halo_col.at[i, depth + 1],
            col_send.at[2, i], col_recv.at[2, i], r - 1, other,
        )

    has_up = r > 0
    has_down = r < rows - 1
    for i in (1, 0):
        tile_mid(i).start()

    @pl.when(has_down)
    def _():
        for i in (1, 0):
            tile_down(i).start()
            down(i).start()

    @pl.when(r == 0)
    def _():
        halo_row[0] = jnp.zeros_like(halo_row[0])
        for i in (0, 1):
            halo_col[i, 0] = jnp.zeros_like(halo_col[i, 0])

    @pl.when(r == rows - 1)
    def _():
        halo_row[1] = jnp.zeros_like(halo_row[1])
        for i in (0, 1):
            halo_col[i, depth + 1] = jnp.zeros_like(halo_col[i, depth + 1])

    spread = [expansion(count, reach, reach // count) for count in (reach, l1.shape[2], l2.shape[1], l3.shape[1])]
    for load in loads:
        load.wait()
    for h in range(depth):
        for s in range(blocks):
            at = pl.ds(s * reach, reach)
            total = matmul(l0[h, at], spread[0], ((1,), (0,)))
            total = total + matmul(l1[h, at], spread[1], ((1,), (0,)))
            for level, way in zip((l2, l3), spread[2:]):
                total = total + matmul(level[h, :, at], way, ((0,), (0,)))
            total = total.astype(BF16).astype(F32)
            wide = jnp.concatenate([total, jnp.zeros_like(total)], axis=1)
            band_m[h, s] = pltpu.roll(wide, 1, 1, stride=1, stride_axis=0).astype(BF16)

    @pl.when(has_down)
    def _():
        for i in (1, 0):
            tile_down(i).wait_send()
            down(i).wait_send()

    @pl.when(has_up)
    def _():
        for i in (1, 0):
            tile_up(i).start()
            up(i).start()

    place = lax.broadcasted_iota(jnp.int32, (band, cin), 0)

    def shifted(x, by, edge):
        if by == 1:
            return jnp.where(place == 0, edge, pltpu.roll(x, 1, 0))
        return jnp.where(place == band - 1, edge, pltpu.roll(x, band - 1, 0))

    def lay(framed, i):
        if framed == 0:
            base = halo_row[0, i]
        elif framed == depth + 1:
            base = halo_row[1, i]
        else:
            base = images[i][framed - 1]
        tile = halo_col[i, framed].astype(F32)
        zero = jnp.zeros((1, cin), F32)
        enter_left = jnp.where(c == 0, zero, tile[TILE - 1 : TILE])
        enter_right = jnp.where(c == 0, tile[0:1], zero)
        wide = base.astype(F32)
        three = (
            shifted(wide, 1, enter_left).astype(BF16),
            base,
            shifted(wide, -1, enter_right).astype(BF16),
        )
        for row_tap in range(3):
            h = framed - row_tap
            if 0 <= h < depth:
                for k in range(3):
                    patch[i, h, :, pl.ds((row_tap * 3 + k) * cin, cin)] = three[k]

    inverse = 1.0 / math.sqrt(features)

    def ext_copy(h):
        return remote(
            right_ext.at[h, pl.ds(band, reach)], right_ext.at[h, pl.ds(0, reach)],
            ext_send.at[h], ext_recv.at[h], r, other,
        )

    def ret_copy(h):
        return remote(ret_out.at[h], ret_in.at[h], ret_send.at[h], ret_recv.at[h], r, other)

    def edge_copy(h):
        return remote(
            grad.at[:, h, pl.ds(near, TILE)], grad_edge.at[:, h], edge_send.at[h], edge_recv.at[h], r, other
        )

    def part_copy(side, i):
        target = r - 1 if side == 0 else r + 1
        return remote(
            part_out.at[side, i], part_in.at[1 - side, i], part_send.at[side, i], part_recv.at[1 - side, i],
            target, c,
        )

    @pl.when(c == 0)
    def _():
        right_ext[:, 0:reach] = jnp.zeros((depth, reach, features), BF16)

    def process(h, ready):
        ready(1)
        feat = matmul(patch[1, h], weight[...], ((1,), (0,)))
        right_ext[h, pl.ds(reach, band)] = feat.astype(BF16)

        @pl.when(c == 0)
        def _():
            ext_copy(h).start()

        ready(0)
        left_feat[...] = matmul(patch[0, h], weight[...], ((1,), (0,))).astype(BF16)
        pending = None
        for s in range(blocks):
            both = matmul(band_m[h, s], left_feat[pl.ds(s * reach, reach)], ((0,), (0,)))
            head = both[:reach]
            if s == 0:
                ret_out[h] = head.astype(BF16)

                @pl.when(c == 1)
                def _():
                    ret_copy(h).start()
            else:
                grad[1, h, pl.ds((s - 1) * reach, reach)] = ((pending + head) * inverse).astype(BF16)
            pending = both[reach:]

        for s in range(blocks - 1, -1, -1):
            if s == 0:

                @pl.when(c == 1)
                def _():
                    ext_copy(h).wait_recv()

            window = right_ext[h, pl.ds(s * reach, 2 * reach)]
            out = matmul(band_m[h, s], window, ((1,), (0,)))
            grad[0, h, pl.ds(s * reach, reach)] = (out * inverse).astype(BF16)

        @pl.when(c == 0)
        def _():
            ret_copy(h).wait_recv()

        came = jnp.where(c == 0, ret_in[h].astype(F32), 0.0)
        grad[1, h, pl.ds(band - reach, reach)] = ((pending + came) * inverse).astype(BF16)
        edge_copy(h).start()
        for i in (0, 1):
            zed[i, h, 0:band] = matmul(grad[i, h], weight[...], ((1,), (1,)))
        edge_copy(h).wait_recv()
        for i in (0, 1):
            zed[i, h, pl.ds(band, TILE)] = matmul(grad_edge[i, h], weight[...], ((1,), (1,)))

    def weight_term(h, k):
        lanes = pl.ds(k * 3 * cin, 3 * cin)
        return matmul(grad[0, h], patch[0, h, :, lanes], ((0,), (0,))) + matmul(
            grad[1, h], patch[1, h, :, lanes], ((0,), (0,))
        )

    def gathered(i, goal):
        total = None
        for b in (0, 1, -1):
            inner = None
            enter = None
            for a in (-1, 0, 1):
                h = goal - a
                if not 0 <= h < depth:
                    continue
                lanes = pl.ds(((a + 1) * 3 + b + 1) * cin, cin)
                main = zed[i, h, 0:band, lanes]
                inner = main if inner is None else inner + main
                if b != 0:
                    line = zed[i, h, pl.ds(band, TILE), lanes]
                    enter = line if enter is None else enter + line
            if b == 0:
                total = inner
            elif b == 1:
                entering = jnp.where(c == 1, enter[TILE - 1 : TILE], 0.0)
                total = total + shifted(inner, 1, entering)
            else:
                entering = jnp.where(c == 0, enter[0:1], 0.0)
                total = total + shifted(inner, -1, entering)
        return total

    for i in (1, 0):
        tile_mid(i).wait_recv()
        for framed in range(1, depth + 1):
            lay(framed, i)

    def from_above(i):
        @pl.when(has_up)
        def _():
            tile_down(i).wait_recv()
            down(i).wait_recv()

        lay(0, i)

    def from_below(i):
        @pl.when(has_down)
        def _():
            tile_up(i).wait_recv()
            up(i).wait_recv()

        lay(depth + 1, i)

    def give(side, goal, allowed):
        for i in (0, 1):
            part_out[side, i] = gathered(i, goal).astype(BF16)

            @pl.when(allowed)
            def _():
                part_copy(side, i).start()

    def entering(h, i):
        if h == 0:
            from_above(i)
        if h == depth - 1:
            from_below(i)

    for h in range(depth):
        process(h, functools.partial(entering, h))
        if h == 0:
            give(0, -1, has_up)
        if h < depth - 1:
            for k in range(3):
                term = weight_term(h, k)
                early[k] = term if h == 0 else early[k] + term
    give(1, depth, has_down)

    scale = 1.0 / math.sqrt(2 * depth * band * group)

    def pair_copy(k):
        return remote(pair_out.at[k, other], pair_in.at[k], pair_send.at[k], pair_recv.at[k], r, other)

    def chunk_copy(k, i):
        target = lax.rem(r + i, rows)
        return remote(
            chunk.at[k, target], landed.at[k, i], chunk_send.at[k, i], chunk_recv.at[k, i], target, c
        )

    for k in range(3):
        total = weight_term(depth - 1, k)
        if depth > 1:
            total = total + early[k]
        total = total * scale
        for s in range(rows):
            for col in range(cols):
                start = (s * cols + col) * quota
                piece = total[start : start + quota]
                acc[k, col, s] = piece
                pair_out[k, col, s] = piece.astype(BF16)
        pair_copy(k).start()
    for k in range(3):
        pair_copy(k).wait_recv()
        for s in range(rows):
            both = acc[k, c, s] + pair_in[k, s].astype(F32)
            acc[k, c, s] = both
            chunk[k, s] = both.astype(BF16)

        def start_chunk(i, carry):
            chunk_copy(k, i).start()
            return carry

        lax.fori_loop(1, rows, start_chunk, 0)

    outs = (gl_out, gr_out)

    def put(goal):
        for i in (0, 1):
            total = gathered(i, goal)
            if goal == 0:
                total = total + jnp.where(has_up, part_in[0, i].astype(F32), 0.0)
            if goal == depth - 1:
                total = total + jnp.where(has_down, part_in[1, i].astype(F32), 0.0)
            outs[i][goal] = total.astype(BF16)

    @pl.when(has_down)
    def _():
        for i in (0, 1):
            part_copy(0, i).wait_recv()

    for goal in range(depth - 1, 0, -1):
        put(goal)

    @pl.when(has_up)
    def _():
        for i in (0, 1):
            part_copy(1, i).wait_recv()

    put(0)

    def last_copy(k):
        return remote(whole.at[k, c], whole.at[k, c], whole_send.at[k], whole_recv.at[k], r, other)

    for k in range(3):

        def wait_chunk(i, carry):
            chunk_copy(k, i).wait_recv()
            return carry

        def add_chunk(i, total):
            return total + landed[k, i].astype(F32)

        lax.fori_loop(1, rows, wait_chunk, 0)
        whole[k, c] = lax.fori_loop(1, rows, add_chunk, acc[k, c, r])
        last_copy(k).start()
    for k in range(3):
        last_copy(k).wait_recv()
        for col in range(cols):
            wg_out[pl.ds(col * quota, quota), pl.ds(k * 3 * cin, 3 * cin)] = whole[k, col]

    for k in range(3):
        last_copy(k).wait_send()
        pair_copy(k).wait_send()

        def drain(i, carry):
            chunk_copy(k, i).wait_send()
            return carry

        lax.fori_loop(1, rows, drain, 0)
    for i in (0, 1):
        tile_mid(i).wait_send()
    for h in range(depth):
        edge_copy(h).wait_send()

    @pl.when(has_down)
    def _():
        for i in (0, 1):
            part_copy(1, i).wait_send()

    @pl.when(has_up)
    def _():
        for i in (0, 1):
            tile_up(i).wait_send()
            up(i).wait_send()
            part_copy(0, i).wait_send()

    @pl.when(c == 0)
    def _():
        for h in range(depth):
            ext_copy(h).wait_send()

    @pl.when(c == 1)
    def _():
        for h in range(depth):
            ret_copy(h).wait_send()


def hand_over(a, b, w, a_out, b_out, w_out, a_mid, b_mid, w_mid, sem_in, sem_out):
    into = [
        pltpu.make_async_copy(src, mid, sem_in.at[k])
        for k, (src, mid) in enumerate(((a, a_mid), (b, b_mid), (w, w_mid)))
    ]
    out = [
        pltpu.make_async_copy(mid, dst, sem_out.at[k])
        for k, (mid, dst) in enumerate(((a_mid, a_out), (b_mid, b_out), (w_mid, w_out)))
    ]
    for copy in into:
        copy.start()
    for first, second in zip(into, out):
        first.wait()
        second.start()
    for copy in out:
        copy.wait()


def on_device(rows, cols, left, right, weight, l0, l1, l2, l3):
    depth, band, cin = left.shape
    taps, features = weight.shape
    reach = l0.shape[2]
    blocks = band // reach
    quota = features // (rows * cols)
    third = taps // 3
    l2 = jnp.swapaxes(l2, 1, 2)
    l3 = jnp.swapaxes(l3, 1, 2)
    vmem = pl.BlockSpec(memory_space=pltpu.VMEM)
    dma = pltpu.SemaphoreType.DMA
    results = pl.pallas_call(
        functools.partial(kernel, rows, cols),
        out_shape=(
            jax.ShapeDtypeStruct(left.shape, BF16),
            jax.ShapeDtypeStruct(right.shape, BF16),
            jax.ShapeDtypeStruct((features // rows, taps), F32),
        ),
        in_specs=[vmem] * 2 + [pl.BlockSpec(memory_space=pl.ANY)] * 5,
        out_specs=(vmem,) * 3,
        scratch_shapes=[
            *(pltpu.VMEM(x.shape, BF16) for x in (weight, l0, l1, l2, l3)),
            pltpu.VMEM((2, 2, band, cin), BF16),
            pltpu.VMEM((2, depth + 2, TILE, cin), BF16),
            pltpu.VMEM((depth, blocks, reach, 2 * reach), BF16),
            pltpu.VMEM((2, depth, band, taps), BF16),
            pltpu.VMEM((band, features), BF16),
            pltpu.VMEM((depth, reach + band, features), BF16),
            pltpu.VMEM((depth, reach, features), BF16),
            pltpu.VMEM((depth, reach, features), BF16),
            pltpu.VMEM((2, depth, band, features), BF16),
            pltpu.VMEM((2, depth, TILE, features), BF16),
            pltpu.VMEM((2, depth, band + TILE, taps), F32),
            pltpu.VMEM((2, 2, band, cin), BF16),
            pltpu.VMEM((2, 2, band, cin), BF16),
            pltpu.VMEM((3, cols, rows, quota, third), F32),
            pltpu.VMEM((3, features, third), F32),
            pltpu.VMEM((3, cols, rows, quota, third), BF16),
            pltpu.VMEM((3, rows, quota, third), BF16),
            pltpu.VMEM((3, rows, quota, third), BF16),
            pltpu.VMEM((3, rows, quota, third), BF16),
            pltpu.VMEM((3, cols, quota, third), F32),
            dma((2, 2)), dma((2, 2)), dma((3, 2)), dma((3, 2)),
            dma((depth,)), dma((depth,)), dma((depth,)), dma((depth,)),
            dma((depth,)), dma((depth,)), dma((2, 2)), dma((2, 2)),
            dma((3,)), dma((3,)), dma((3, rows)), dma((3, rows)), dma((3,)), dma((3,)), dma((5,)),
        ],
        compiler_params=pltpu.CompilerParams(
            collective_id=0, has_side_effects=True, vmem_limit_bytes=60 * 1024 * 1024
        ),
        name="stereo_backward",
    )(left, right, weight, l0, l1, l2, l3)
    hbm = pl.BlockSpec(memory_space=pl.ANY)
    shapes = tuple(jax.ShapeDtypeStruct(x.shape, x.dtype) for x in results)
    return pl.pallas_call(
        hand_over,
        out_shape=shapes,
        in_specs=[hbm] * 3,
        out_specs=(hbm,) * 3,
        scratch_shapes=[*(pltpu.VMEM(x.shape, x.dtype) for x in results), dma((3,)), dma((3,))],
        name="hand_over",
    )(*results)


def solution(mesh):
    banded = P(("pairs", "rows"), "cols", None)
    return jax.shard_map(
        functools.partial(on_device, mesh.shape["rows"], mesh.shape["cols"]),
        mesh=mesh,
        in_specs=(banded, banded, P(), banded, banded, banded, banded),
        out_specs=(banded, banded, P(("pairs", "rows"), None)),
        check_vma=False,
    )
```

profile of v0, /device:TPU:29, one launch (start us, length us, event | category | flops | bytes accessed | tf_op | source)
XLA Modules:
  0.0 41.6 jit_solution(17383441532434350496)
XLA Ops:
  0.6 39.2 %stereo_backward.1 = (bf16[2,512,128]{2,1,0:T(8,128)(2,1)}, bf16[2,512,128]{2,1,0:T(8,128)(2,1)}, f32[32,1152]{1,0:T(8,128)}) custom-call(bf16[2,512,128]{2,1,0:T(8,128)(2,1)} %left.1, bf16[2,512,128]{2,1,0:T(8,128)(2,1)} %right.1, bf16[1152,256]{1,0:T(8,128)(2,1)} %weight_hbm.1, bf16[2,512,256]{2,1,0:T(8,128)(2,1)} %l0_hbm.1, bf16[2,512,128]{2,1,0:T(8,128)(2,1)} %l1_hbm.1, ...), custom_call_target="tpu_custom_call" | custom-call | tf_op jit(solution)/shard_map/stereo_backward/pallas_call | solution.py:486
  39.8 1.8 %hand_over.1 = (bf16[2,512,128]{2,1,0:T(8,128)(2,1)}, bf16[2,512,128]{2,1,0:T(8,128)(2,1)}, f32[32,1152]{1,0:T(8,128)}) custom-call(bf16[2,512,128]{2,1,0:T(8,128)(2,1)} %get-tuple-element.6.a, bf16[2,512,128]{2,1,0:T(8,128)(2,1)} %get-tuple-element.7.b, f32[32,1152]{1,0:T(8,128)} %get-tuple-element.8.w), custom_call_target="tpu_custom_call" | custom-call | tf_op jit(solution)/shard_map/hand_over/pallas_call | solution.py:529
where the time goes:
time: 41.8 us; the launch traced here: 41.6 us
  Pallas kernels  41 us (98%)
  between operations  0.64 us (2%)
    pallas_call x1, Pallas kernels, on_device(): pl.pallas_call(functools.partial(kernel, rows, cols), out_shape=(jax.Shap...  39.2 us
    pallas_call x1, Pallas kernels, on_device(): pl.pallas_call(hand_over, out_shape=shapes, in_specs=[hbm] * 3, out_specs...  1.84 us

commit v1 on v0

--- a/solution.py
+++ b/solution.py
@@ -37,11 +37,11 @@
 
 
 def kernel(
-    rows, cols, left, right, weight_hbm, l0_hbm, l1_hbm, l2_hbm, l3_hbm, gl_out, gr_out, wg_out,
-    weight, l0, l1, l2, l3, halo_row, halo_col, band_m, patch, left_feat, right_ext, ret_out, ret_in,
+    rows, cols, left_hbm, right_hbm, weight_hbm, l0_hbm, l1_hbm, l2_hbm, l3_hbm, gl_out, gr_out, wg_out,
+    left, right, gl_buf, gr_buf, wg_buf, weight, l0, l1, l2, l3, halo_row, halo_col, band_m, patch, left_feat, right_ext, ret_out, ret_in,
     grad, grad_edge, zed, part_out, part_in, acc, early, pair_out, pair_in, chunk, landed, whole,
     row_send, row_recv, col_send, col_recv, ext_send, ext_recv, ret_send, ret_recv,
-    edge_send, edge_recv, part_send, part_recv, pair_send, pair_recv, chunk_send, chunk_recv, whole_send, whole_recv, load_sem,
+    edge_send, edge_recv, part_send, part_recv, pair_send, pair_recv, chunk_send, chunk_recv, whole_send, whole_recv, load_sem, store_sem, known,
 ):
     depth, band, cin = left.shape
     features = weight.shape[1]
@@ -52,60 +52,89 @@
     c = lax.axis_index("cols")
     other = 1 - c
     images = (left, right)
+    sources = (left_hbm, right_hbm)
     group = rows * cols
-    me = r * cols + c
+    has_up = r > 0
+    has_down = r < rows - 1
 
     barrier = pltpu.get_barrier_semaphore()
 
-    def greet(i, carry):
-        peer = lax.rem(me + i, group)
+    def tell(semaphore, row, col):
         pl.semaphore_signal(
-            barrier,
-            inc=1,
-            device_id={"rows": peer // cols, "cols": lax.rem(peer, cols)},
-            device_id_type=pl.DeviceIdType.MESH,
-        )
-        return carry
-
-    lax.fori_loop(1, group, greet, 0)
+            semaphore, inc=1, device_id={"rows": row, "cols": col}, device_id_type=pl.DeviceIdType.MESH
+        )
+
+    tell(barrier, r, other)
+
+    @pl.when(has_up)
+    def _():
+        for col in (c, other):
+            tell(barrier, r - 1, col)
+
+    @pl.when(has_down)
+    def _():
+        for col in (c, other):
+            tell(barrier, r + 1, col)
+
     loads = [
         pltpu.make_async_copy(src, dst, load_sem.at[k])
         for k, (src, dst) in enumerate(
-            ((l0_hbm, l0), (l1_hbm, l1), (l2_hbm, l2), (l3_hbm, l3), (weight_hbm, weight))
+            (
+                (l0_hbm, l0), (l1_hbm, l1), (l2_hbm, l2), (l3_hbm, l3),
+                (right_hbm, right), (left_hbm, left), (weight_hbm, weight),
+            )
         )
     ]
     for load in loads:
         load.start()
-    pl.semaphore_wait(barrier, group - 1)
+    pl.semaphore_wait(barrier, 1 + 2 * has_up.astype(jnp.int32) + 2 * has_down.astype(jnp.int32))
+
+    rounds = (rows - 1).bit_length()
+
+    def spread_word(k):
+        @pl.when(r >= 2**k)
+        def _():
+            tell(known.at[k, 1], r - 2**k, c)
+
+        @pl.when(r + 2**k < rows)
+        def _():
+            tell(known.at[k, 0], r + 2**k, c)
+
+    def hear_word(k):
+        @pl.when(r >= 2**k)
+        def _():
+            pl.semaphore_wait(known.at[k, 0], 1)
+
+        @pl.when(r + 2**k < rows)
+        def _():
+            pl.semaphore_wait(known.at[k, 1], 1)
 
     near = pl.multiple_of(other * (band - TILE), TILE)
 
     def down(i):
-        return remote(images[i].at[depth - 1], halo_row.at[0, i], row_send.at[0, i], row_recv.at[0, i], r + 1, c)
+        return remote(sources[i].at[depth - 1], halo_row.at[0, i], row_send.at[0, i], row_recv.at[0, i], r + 1, c)
 
     def up(i):
-        return remote(images[i].at[0], halo_row.at[1, i], row_send.at[1, i], row_recv.at[1, i], r - 1, c)
+        return remote(sources[i].at[0], halo_row.at[1, i], row_send.at[1, i], row_recv.at[1, i], r - 1, c)
 
     def tile_mid(i):
         return remote(
-            images[i].at[:, pl.ds(near, TILE)], halo_col.at[i, pl.ds(1, depth)],
+            sources[i].at[:, pl.ds(near, TILE)], halo_col.at[i, pl.ds(1, depth)],
             col_send.at[0, i], col_recv.at[0, i], r, other,
         )
 
     def tile_down(i):
         return remote(
-            images[i].at[depth - 1, pl.ds(near, TILE)], halo_col.at[i, 0],
+            sources[i].at[depth - 1, pl.ds(near, TILE)], halo_col.at[i, 0],
             col_send.at[1, i], col_recv.at[1, i], r + 1, other,
         )
 
     def tile_up(i):
         return remote(
-            images[i].at[0, pl.ds(near, TILE)], halo_col.at[i, depth + 1],
+            sources[i].at[0, pl.ds(near, TILE)], halo_col.at[i, depth + 1],
             col_send.at[2, i], col_recv.at[2, i], r - 1, other,
         )
 
-    has_up = r > 0
-    has_down = r < rows - 1
     for i in (1, 0):
         tile_mid(i).start()
 
@@ -115,6 +144,8 @@
             tile_down(i).start()
             down(i).start()
 
+    spread_word(0)
+
     @pl.when(r == 0)
     def _():
         halo_row[0] = jnp.zeros_like(halo_row[0])
@@ -128,7 +159,7 @@
             halo_col[i, depth + 1] = jnp.zeros_like(halo_col[i, depth + 1])
 
     spread = [expansion(count, reach, reach // count) for count in (reach, l1.shape[2], l2.shape[1], l3.shape[1])]
-    for load in loads:
+    for load in loads[:4]:
         load.wait()
     for h in range(depth):
         for s in range(blocks):
@@ -140,18 +171,6 @@
             total = total.astype(BF16).astype(F32)
             wide = jnp.concatenate([total, jnp.zeros_like(total)], axis=1)
             band_m[h, s] = pltpu.roll(wide, 1, 1, stride=1, stride_axis=0).astype(BF16)
-
-    @pl.when(has_down)
-    def _():
-        for i in (1, 0):
-            tile_down(i).wait_send()
-            down(i).wait_send()
-
-    @pl.when(has_up)
-    def _():
-        for i in (1, 0):
-            tile_up(i).start()
-            up(i).start()
 
     place = lax.broadcasted_iota(jnp.int32, (band, cin), 0)
 
@@ -182,6 +201,29 @@
             if 0 <= h < depth:
                 for k in range(3):
                     patch[i, h, :, pl.ds((row_tap * 3 + k) * cin, cin)] = three[k]
+
+    for load in loads[4:]:
+        load.wait()
+    for i in (1, 0):
+        tile_mid(i).wait_recv()
+        for framed in range(1, depth + 1):
+            lay(framed, i)
+
+    @pl.when(has_down)
+    def _():
+        for i in (1, 0):
+            tile_down(i).wait_send()
+            down(i).wait_send()
+
+    @pl.when(has_up)
+    def _():
+        for i in (1, 0):
+            tile_up(i).start()
+            up(i).start()
+
+    hear_word(0)
+    if rounds > 1:
+        spread_word(1)
 
     inverse = 1.0 / math.sqrt(features)
 
@@ -290,11 +332,6 @@
                 total = total + shifted(inner, -1, entering)
         return total
 
-    for i in (1, 0):
-        tile_mid(i).wait_recv()
-        for framed in range(1, depth + 1):
-            lay(framed, i)
-
     def from_above(i):
         @pl.when(has_up)
         def _():
@@ -329,11 +366,20 @@
         process(h, functools.partial(entering, h))
         if h == 0:
             give(0, -1, has_up)
+            if rounds > 1:
+                hear_word(1)
+            if rounds > 2:
+                spread_word(2)
         if h < depth - 1:
             for k in range(3):
                 term = weight_term(h, k)
                 early[k] = term if h == 0 else early[k] + term
     give(1, depth, has_down)
+
+    for k in range(2, rounds):
+        hear_word(k)
+        if k + 1 < rounds:
+            spread_word(k + 1)
 
     scale = 1.0 / math.sqrt(2 * depth * band * group)
 
@@ -371,7 +417,10 @@
 
         lax.fori_loop(1, rows, start_chunk, 0)
 
-    outs = (gl_out, gr_out)
+    outs = (gl_buf, gr_buf)
+
+    def store(i, goal):
+        return pltpu.make_async_copy(outs[i].at[goal], (gl_out, gr_out)[i].at[goal], store_sem.at[i, goal])
 
     def put(goal):
         for i in (0, 1):
@@ -381,6 +430,7 @@
             if goal == depth - 1:
                 total = total + jnp.where(has_down, part_in[1, i].astype(F32), 0.0)
             outs[i][goal] = total.astype(BF16)
+            store(i, goal).start()
 
     @pl.when(has_down)
     def _():
@@ -415,8 +465,10 @@
     for k in range(3):
         last_copy(k).wait_recv()
         for col in range(cols):
-            wg_out[pl.ds(col * quota, quota), pl.ds(k * 3 * cin, 3 * cin)] = whole[k, col]
-
+            wg_buf[pl.ds(col * quota, quota), pl.ds(k * 3 * cin, 3 * cin)] = whole[k, col]
+
+    whole_store = pltpu.make_async_copy(wg_buf, wg_out, load_sem.at[0])
+    whole_store.start()
     for k in range(3):
         last_copy(k).wait_send()
         pair_copy(k).wait_send()
@@ -452,6 +504,11 @@
     def _():
         for h in range(depth):
             ret_copy(h).wait_send()
+
+    for i in (0, 1):
+        for goal in range(depth):
+            store(i, goal).wait()
+    whole_store.wait()
 
 
 def hand_over(a, b, w, a_out, b_out, w_out, a_mid, b_mid, w_mid, sem_in, sem_out):
@@ -481,7 +538,6 @@
     third = taps // 3
     l2 = jnp.swapaxes(l2, 1, 2)
     l3 = jnp.swapaxes(l3, 1, 2)
-    vmem = pl.BlockSpec(memory_space=pltpu.VMEM)
     dma = pltpu.SemaphoreType.DMA
     results = pl.pallas_call(
         functools.partial(kernel, rows, cols),
@@ -490,9 +546,11 @@
             jax.ShapeDtypeStruct(right.shape, BF16),
             jax.ShapeDtypeStruct((features // rows, taps), F32),
         ),
-        in_specs=[vmem] * 2 + [pl.BlockSpec(memory_space=pl.ANY)] * 5,
-        out_specs=(vmem,) * 3,
+        in_specs=[pl.BlockSpec(memory_space=pl.ANY)] * 7,
+        out_specs=(pl.BlockSpec(memory_space=pl.ANY),) * 3,
         scratch_shapes=[
+            *(pltpu.VMEM(x.shape, BF16) for x in (left, right, left, right)),
+            pltpu.VMEM((features // rows, taps), F32),
             *(pltpu.VMEM(x.shape, BF16) for x in (weight, l0, l1, l2, l3)),
             pltpu.VMEM((2, 2, band, cin), BF16),
             pltpu.VMEM((2, depth + 2, TILE, cin), BF16),
@@ -517,7 +575,8 @@
             dma((2, 2)), dma((2, 2)), dma((3, 2)), dma((3, 2)),
             dma((depth,)), dma((depth,)), dma((depth,)), dma((depth,)),
             dma((depth,)), dma((depth,)), dma((2, 2)), dma((2, 2)),
-            dma((3,)), dma((3,)), dma((3, rows)), dma((3, rows)), dma((3,)), dma((3,)), dma((5,)),
+            dma((3,)), dma((3,)), dma((3, rows)), dma((3, rows)), dma((3,)), dma((3,)), dma((7,)),
+            dma((2, depth)), pltpu.SemaphoreType.REGULAR(((rows - 1).bit_length(), 2)),
         ],
         compiler_params=pltpu.CompilerParams(
             collective_id=0, has_side_effects=True, vmem_limit_bytes=60 * 1024 * 1024

time: 41.8 us -> 40.5 us (0.969)
  Pallas kernels: 41 us -> 39.7 us
    pallas_call x1, Pallas kernels: 39.2 us -> 37.9 us  [on_device(): pl.pallas_call(functools.partial(kernel, rows, cols), out_shape=(jax.Shap...]
where the time goes in v1:
time: 40.5 us; the launch traced here: 40.4 us
  Pallas kernels  39.7 us (98%)
  between operations  0.64 us (2%)
    pallas_call x1, Pallas kernels, on_device(): pl.pallas_call(functools.partial(kernel, rows, cols), out_shape=(jax.Shap...  37.9 us
    pallas_call x1, Pallas kernels, on_device(): pl.pallas_call(hand_over, out_shape=shapes, in_specs=[hbm] * 3, out_specs...  1.84 us

profile of v1, /device:TPU:29, one launch (start us, length us, event | category | flops | bytes accessed | tf_op | source)
XLA Modules:
  0.0 40.4 jit_solution(10936203733862023877)
XLA Ops:
  0.6 37.9 %stereo_backward.1 = (bf16[2,512,128]{2,1,0:T(8,128)(2,1)}, bf16[2,512,128]{2,1,0:T(8,128)(2,1)}, f32[32,1152]{1,0:T(8,128)}) custom-call(bf16[2,512,128]{2,1,0:T(8,128)(2,1)} %left_hbm.1, bf16[2,512,128]{2,1,0:T(8,128)(2,1)} %right_hbm.1, bf16[1152,256]{1,0:T(8,128)(2,1)} %weight_hbm.1, bf16[2,512,256]{2,1,0:T(8,128)(2,1)} %l0_hbm.1, ...), custom_call_target="tpu_custom_call" | custom-call | tf_op jit(solution)/shard_map/stereo_backward/pallas_call | solution.py:542
  38.5 1.8 %hand_over.1 = (bf16[2,512,128]{2,1,0:T(8,128)(2,1)}, bf16[2,512,128]{2,1,0:T(8,128)(2,1)}, f32[32,1152]{1,0:T(8,128)}) custom-call(bf16[2,512,128]{2,1,0:T(8,128)(2,1)} %get-tuple-element.6.a, bf16[2,512,128]{2,1,0:T(8,128)(2,1)} %get-tuple-element.7.b, f32[32,1152]{1,0:T(8,128)} %get-tuple-element.8.w), custom_call_target="tpu_custom_call" | custom-call | tf_op jit(solution)/shard_map/hand_over/pallas_call | solution.py:588

commit v2 on v1

--- a/solution.py
+++ b/solution.py
@@ -39,9 +39,9 @@
 def kernel(
     rows, cols, left_hbm, right_hbm, weight_hbm, l0_hbm, l1_hbm, l2_hbm, l3_hbm, gl_out, gr_out, wg_out,
     left, right, gl_buf, gr_buf, wg_buf, weight, l0, l1, l2, l3, halo_row, halo_col, band_m, patch, left_feat, right_ext, ret_out, ret_in,
-    grad, grad_edge, zed, part_out, part_in, acc, early, pair_out, pair_in, chunk, landed, whole,
+    grad, grad_edge, zed, part_out, part_in, own_conv, acc, early, pair_out, pair_in, cross_out, cross_in, chunk, landed, whole,
     row_send, row_recv, col_send, col_recv, ext_send, ext_recv, ret_send, ret_recv,
-    edge_send, edge_recv, part_send, part_recv, pair_send, pair_recv, chunk_send, chunk_recv, whole_send, whole_recv, load_sem, store_sem, known,
+    edge_send, edge_recv, part_send, part_recv, pair_send, pair_recv, cross_send, cross_recv, chunk_send, chunk_recv, whole_send, whole_recv, load_sem, store_sem, known,
 ):
     depth, band, cin = left.shape
     features = weight.shape[1]
@@ -202,29 +202,6 @@
                 for k in range(3):
                     patch[i, h, :, pl.ds((row_tap * 3 + k) * cin, cin)] = three[k]
 
-    for load in loads[4:]:
-        load.wait()
-    for i in (1, 0):
-        tile_mid(i).wait_recv()
-        for framed in range(1, depth + 1):
-            lay(framed, i)
-
-    @pl.when(has_down)
-    def _():
-        for i in (1, 0):
-            tile_down(i).wait_send()
-            down(i).wait_send()
-
-    @pl.when(has_up)
-    def _():
-        for i in (1, 0):
-            tile_up(i).start()
-            up(i).start()
-
-    hear_word(0)
-    if rounds > 1:
-        spread_word(1)
-
     inverse = 1.0 / math.sqrt(features)
 
     def ext_copy(h):
@@ -236,9 +213,9 @@
     def ret_copy(h):
         return remote(ret_out.at[h], ret_in.at[h], ret_send.at[h], ret_recv.at[h], r, other)
 
-    def edge_copy(h):
+    def edge_copy(h, i):
         return remote(
-            grad.at[:, h, pl.ds(near, TILE)], grad_edge.at[:, h], edge_send.at[h], edge_recv.at[h], r, other
+            grad.at[i, h, pl.ds(near, TILE)], grad_edge.at[i, h], edge_send.at[i, h], edge_recv.at[i, h], r, other
         )
 
     def part_copy(side, i):
@@ -252,17 +229,55 @@
     def _():
         right_ext[:, 0:reach] = jnp.zeros((depth, reach, features), BF16)
 
-    def process(h, ready):
-        ready(1)
-        feat = matmul(patch[1, h], weight[...], ((1,), (0,)))
-        right_ext[h, pl.ds(reach, band)] = feat.astype(BF16)
+    def own_taps(h):
+        return (0 if h > 0 else 1), (3 if h < depth - 1 else 2)
+
+    def convolve(i, h, first, last):
+        lanes = pl.ds(first * 3 * cin, (last - first) * 3 * cin)
+        return matmul(patch[i, h, :, lanes], weight[lanes], ((1,), (0,)))
+
+    def feature(i, h):
+        first, last = own_taps(h)
+        total = own_conv[i, h]
+        if first > 0:
+            total = total + convolve(i, h, 0, first)
+        if last < 3:
+            total = total + convolve(i, h, last, 3)
+        return total.astype(BF16)
+
+    def weight_term(i, h):
+        return matmul(grad[i, h], patch[i, h], ((0,), (0,)))
+
+    def spread_grad(i, h):
+        zed[i, h, 0:band] = matmul(grad[i, h], weight[...], ((1,), (1,)))
+
+    def spread_edge(i, h):
+        edge_copy(h, i).wait_recv()
+        zed[i, h, pl.ds(band, TILE)] = matmul(grad_edge[i, h], weight[...], ((1,), (1,)))
+
+    def left_chain(h):
+        right_ext[h, pl.ds(reach, band)] = feature(1, h)
 
         @pl.when(c == 0)
         def _():
             ext_copy(h).start()
 
-        ready(0)
-        left_feat[...] = matmul(patch[0, h], weight[...], ((1,), (0,))).astype(BF16)
+        for s in range(blocks - 1, -1, -1):
+            if s == 0:
+
+                @pl.when(c == 1)
+                def _():
+                    ext_copy(h).wait_recv()
+
+            window = right_ext[h, pl.ds(s * reach, 2 * reach)]
+            out = matmul(band_m[h, s], window, ((1,), (0,)))
+            grad[0, h, pl.ds(s * reach, reach)] = (out * inverse).astype(BF16)
+        edge_copy(h, 0).start()
+        spread_grad(0, h)
+        spread_edge(0, h)
+
+    def right_chain(h):
+        left_feat[...] = feature(0, h)
         pending = None
         for s in range(blocks):
             both = matmul(band_m[h, s], left_feat[pl.ds(s * reach, reach)], ((0,), (0,)))
@@ -277,16 +292,10 @@
                 grad[1, h, pl.ds((s - 1) * reach, reach)] = ((pending + head) * inverse).astype(BF16)
             pending = both[reach:]
 
-        for s in range(blocks - 1, -1, -1):
-            if s == 0:
-
-                @pl.when(c == 1)
-                def _():
-                    ext_copy(h).wait_recv()
-
-            window = right_ext[h, pl.ds(s * reach, 2 * reach)]
-            out = matmul(band_m[h, s], window, ((1,), (0,)))
-            grad[0, h, pl.ds(s * reach, reach)] = (out * inverse).astype(BF16)
+        if h == 0:
+            early[...] = weight_term(0, h)
+        else:
+            early[...] += weight_term(0, h)
 
         @pl.when(c == 0)
         def _():
@@ -294,18 +303,7 @@
 
         came = jnp.where(c == 0, ret_in[h].astype(F32), 0.0)
         grad[1, h, pl.ds(band - reach, reach)] = ((pending + came) * inverse).astype(BF16)
-        edge_copy(h).start()
-        for i in (0, 1):
-            zed[i, h, 0:band] = matmul(grad[i, h], weight[...], ((1,), (1,)))
-        edge_copy(h).wait_recv()
-        for i in (0, 1):
-            zed[i, h, pl.ds(band, TILE)] = matmul(grad_edge[i, h], weight[...], ((1,), (1,)))
-
-    def weight_term(h, k):
-        lanes = pl.ds(k * 3 * cin, 3 * cin)
-        return matmul(grad[0, h], patch[0, h, :, lanes], ((0,), (0,))) + matmul(
-            grad[1, h], patch[1, h, :, lanes], ((0,), (0,))
-        )
+        edge_copy(h, 1).start()
 
     def gathered(i, goal):
         total = None
@@ -332,6 +330,32 @@
                 total = total + shifted(inner, -1, entering)
         return total
 
+    for load in loads[4:]:
+        load.wait()
+    for i in (1, 0):
+        tile_mid(i).wait_recv()
+        for framed in range(1, depth + 1):
+            lay(framed, i)
+    for i in (1, 0):
+        for h in range(depth):
+            own_conv[i, h] = convolve(i, h, *own_taps(h))
+
+    @pl.when(has_down)
+    def _():
+        for i in (1, 0):
+            tile_down(i).wait_send()
+            down(i).wait_send()
+
+    @pl.when(has_up)
+    def _():
+        for i in (1, 0):
+            tile_up(i).start()
+            up(i).start()
+
+    hear_word(0)
+    if rounds > 1:
+        spread_word(1)
+
     def from_above(i):
         @pl.when(has_up)
         def _():
@@ -348,13 +372,12 @@
 
         lay(depth + 1, i)
 
-    def give(side, goal, allowed):
-        for i in (0, 1):
-            part_out[side, i] = gathered(i, goal).astype(BF16)
-
-            @pl.when(allowed)
-            def _():
-                part_copy(side, i).start()
+    def give(side, goal, allowed, i):
+        part_out[side, i] = gathered(i, goal).astype(BF16)
+
+        @pl.when(allowed)
+        def _():
+            part_copy(side, i).start()
 
     def entering(h, i):
         if h == 0:
@@ -362,60 +385,63 @@
         if h == depth - 1:
             from_below(i)
 
+    def pair_copy(k):
+        return remote(pair_out.at[k, other], pair_in.at[k], pair_send.at[k], pair_recv.at[k], r, other)
+
+    scale = 1.0 / math.sqrt(2 * depth * band * group)
     for h in range(depth):
-        process(h, functools.partial(entering, h))
+        entering(h, 1)
+        left_chain(h)
+        entering(h, 0)
+        right_chain(h)
+        if h < depth - 1:
+            early[...] += weight_term(1, h)
+        else:
+            for k in range(3):
+                lanes = pl.ds(k * 3 * cin, 3 * cin)
+                total = matmul(grad[1, h], patch[1, h, :, lanes], ((0,), (0,)))
+                total = (early[:, lanes] + total) * scale
+                for s in range(rows):
+                    for col in range(cols):
+                        start = (s * cols + col) * quota
+                        piece = total[start : start + quota]
+                        acc[k, col, s % 2, s // 2] = piece
+                        pair_out[k, col, s % 2, s // 2] = piece.astype(BF16)
+                pair_copy(k).start()
+        spread_grad(1, h)
+        spread_edge(1, h)
         if h == 0:
-            give(0, -1, has_up)
+            for i in (0, 1):
+                give(0, -1, has_up, i)
             if rounds > 1:
                 hear_word(1)
             if rounds > 2:
                 spread_word(2)
-        if h < depth - 1:
-            for k in range(3):
-                term = weight_term(h, k)
-                early[k] = term if h == 0 else early[k] + term
-    give(1, depth, has_down)
-
     for k in range(2, rounds):
         hear_word(k)
         if k + 1 < rounds:
             spread_word(k + 1)
 
-    scale = 1.0 / math.sqrt(2 * depth * band * group)
-
-    def pair_copy(k):
-        return remote(pair_out.at[k, other], pair_in.at[k], pair_send.at[k], pair_recv.at[k], r, other)
+    half = rows // 2
+    place_in_half = r // 2
+    parity = lax.rem(r, 2)
+    across = r + 1 - 2 * parity
+
+    def cross_copy(k):
+        return remote(cross_out.at[k], cross_in.at[k], cross_send.at[k], cross_recv.at[k], across, c)
 
     def chunk_copy(k, i):
-        target = lax.rem(r + i, rows)
+        goal = lax.rem(place_in_half + i, half)
         return remote(
-            chunk.at[k, target], landed.at[k, i], chunk_send.at[k, i], chunk_recv.at[k, i], target, c
-        )
-
-    for k in range(3):
-        total = weight_term(depth - 1, k)
-        if depth > 1:
-            total = total + early[k]
-        total = total * scale
-        for s in range(rows):
-            for col in range(cols):
-                start = (s * cols + col) * quota
-                piece = total[start : start + quota]
-                acc[k, col, s] = piece
-                pair_out[k, col, s] = piece.astype(BF16)
-        pair_copy(k).start()
+            chunk.at[k, goal], landed.at[k, i], chunk_send.at[k, i], chunk_recv.at[k, i], 2 * goal + parity, c
+        )
+
     for k in range(3):
         pair_copy(k).wait_recv()
-        for s in range(rows):
-            both = acc[k, c, s] + pair_in[k, s].astype(F32)
-            acc[k, c, s] = both
-            chunk[k, s] = both.astype(BF16)
-
-        def start_chunk(i, carry):
-            chunk_copy(k, i).start()
-            return carry
-
-        lax.fori_loop(1, rows, start_chunk, 0)
+        cross_out[k] = (acc[k, c, 1 - parity] + pair_in[k, 1 - parity].astype(F32)).astype(BF16)
+        cross_copy(k).start()
+        acc[k, c, parity] += pair_in[k, parity].astype(F32)
+
 
     outs = (gl_buf, gr_buf)
 
@@ -432,6 +458,24 @@
             outs[i][goal] = total.astype(BF16)
             store(i, goal).start()
 
+    def last_copy(k):
+        return remote(whole.at[k, c], whole.at[k, c], whole_send.at[k], whole_recv.at[k], r, other)
+
+    for k in range(3):
+        cross_copy(k).wait_recv()
+        total = acc[k, c, parity] + cross_in[k].astype(F32)
+        acc[k, c, parity] = total
+        chunk[k] = total.astype(BF16)
+
+        def start_chunk(i, carry):
+            chunk_copy(k, i).start()
+            return carry
+
+        lax.fori_loop(1, half, start_chunk, 0)
+
+    for i in (0, 1):
+        give(1, depth, has_down, i)
+
     @pl.when(has_down)
     def _():
         for i in (0, 1):
@@ -439,16 +483,6 @@
 
     for goal in range(depth - 1, 0, -1):
         put(goal)
-
-    @pl.when(has_up)
-    def _():
-        for i in (0, 1):
-            part_copy(1, i).wait_recv()
-
-    put(0)
-
-    def last_copy(k):
-        return remote(whole.at[k, c], whole.at[k, c], whole_send.at[k], whole_recv.at[k], r, other)
 
     for k in range(3):
 
@@ -459,9 +493,17 @@
         def add_chunk(i, total):
             return total + landed[k, i].astype(F32)
 
-        lax.fori_loop(1, rows, wait_chunk, 0)
-        whole[k, c] = lax.fori_loop(1, rows, add_chunk, acc[k, c, r])
+        lax.fori_loop(1, half, wait_chunk, 0)
+        whole[k, c] = lax.fori_loop(1, half, add_chunk, acc[k, c, parity, place_in_half])
         last_copy(k).start()
+
+    @pl.when(has_up)
+    def _():
+        for i in (0, 1):
+            part_copy(1, i).wait_recv()
+
+    put(0)
+
     for k in range(3):
         last_copy(k).wait_recv()
         for col in range(cols):
@@ -472,16 +514,18 @@
     for k in range(3):
         last_copy(k).wait_send()
         pair_copy(k).wait_send()
+        cross_copy(k).wait_send()
 
         def drain(i, carry):
             chunk_copy(k, i).wait_send()
             return carry
 
-        lax.fori_loop(1, rows, drain, 0)
+        lax.fori_loop(1, half, drain, 0)
     for i in (0, 1):
         tile_mid(i).wait_send()
     for h in range(depth):
-        edge_copy(h).wait_send()
+        for i in (0, 1):
+            edge_copy(h, i).wait_send()
 
     @pl.when(has_down)
     def _():
@@ -565,17 +609,17 @@
             pltpu.VMEM((2, depth, band + TILE, taps), F32),
             pltpu.VMEM((2, 2, band, cin), BF16),
             pltpu.VMEM((2, 2, band, cin), BF16),
-            pltpu.VMEM((3, cols, rows, quota, third), F32),
-            pltpu.VMEM((3, features, third), F32),
-            pltpu.VMEM((3, cols, rows, quota, third), BF16),
-            pltpu.VMEM((3, rows, quota, third), BF16),
-            pltpu.VMEM((3, rows, quota, third), BF16),
-            pltpu.VMEM((3, rows, quota, third), BF16),
+            pltpu.VMEM((2, depth, band, features), F32),
+            pltpu.VMEM((3, cols, 2, rows // 2, quota, third), F32),
+            pltpu.VMEM((features, taps), F32),
+            pltpu.VMEM((3, cols, 2, rows // 2, quota, third), BF16),
+            pltpu.VMEM((3, 2, rows // 2, quota, third), BF16),
+            *(pltpu.VMEM((3, rows // 2, quota, third), BF16) for _ in range(4)),
             pltpu.VMEM((3, cols, quota, third), F32),
             dma((2, 2)), dma((2, 2)), dma((3, 2)), dma((3, 2)),
             dma((depth,)), dma((depth,)), dma((depth,)), dma((depth,)),
-            dma((depth,)), dma((depth,)), dma((2, 2)), dma((2, 2)),
-            dma((3,)), dma((3,)), dma((3, rows)), dma((3, rows)), dma((3,)), dma((3,)), dma((7,)),
+            dma((2, depth)), dma((2, depth)), dma((2, 2)), dma((2, 2)),
+            dma((3,)), dma((3,)), dma((3,)), dma((3,)), dma((3, rows // 2)), dma((3, rows // 2)), dma((3,)), dma((3,)), dma((7,)),
             dma((2, depth)), pltpu.SemaphoreType.REGULAR(((rows - 1).bit_length(), 2)),
         ],
         compiler_params=pltpu.CompilerParams(

time: 40.5 us -> 39 us (0.963)
  the two profiles are of different devices: /device:TPU:29 before, /device:TPU:16 now
where the time goes in v2:
time: 39 us; the launch traced here: 38.8 us
  Pallas kernels  38.2 us (98%)
  between operations  0.64 us (2%)
    pallas_call x1, Pallas kernels, on_device(): pl.pallas_call(functools.partial(kernel, rows, cols), out_shape=(jax.Shap...  36.3 us
    pallas_call x1, Pallas kernels, on_device(): pl.pallas_call(hand_over, out_shape=shapes, in_specs=[hbm] * 3, out_specs...  1.84 us

profile of v2, /device:TPU:16, one launch (start us, length us, event | category | flops | bytes accessed | tf_op | source)
XLA Modules:
  0.0 38.8 jit_solution(2446601299863129010)
XLA Ops:
  0.6 36.3 %stereo_backward.1 = (bf16[2,512,128]{2,1,0:T(8,128)(2,1)}, bf16[2,512,128]{2,1,0:T(8,128)(2,1)}, f32[32,1152]{1,0:T(8,128)}) custom-call(bf16[2,512,128]{2,1,0:T(8,128)(2,1)} %left_hbm.1, bf16[2,512,128]{2,1,0:T(8,128)(2,1)} %right_hbm.1, bf16[1152,256]{1,0:T(8,128)(2,1)} %weight_hbm.1, bf16[2,512,256]{2,1,0:T(8,128)(2,1)} %l0_hbm.1, ...), custom_call_target="tpu_custom_call" | custom-call | tf_op jit(solution)/shard_map/stereo_backward/pallas_call | solution.py:586
  37.0 1.8 %hand_over.1 = (bf16[2,512,128]{2,1,0:T(8,128)(2,1)}, bf16[2,512,128]{2,1,0:T(8,128)(2,1)}, f32[32,1152]{1,0:T(8,128)}) custom-call(bf16[2,512,128]{2,1,0:T(8,128)(2,1)} %get-tuple-element.6.a, bf16[2,512,128]{2,1,0:T(8,128)(2,1)} %get-tuple-element.7.b, f32[32,1152]{1,0:T(8,128)} %get-tuple-element.8.w), custom_call_target="tpu_custom_call" | custom-call | tf_op jit(solution)/shard_map/hand_over/pallas_call | solution.py:632

commit v3 on v2

--- a/solution.py
+++ b/solution.py
@@ -264,6 +264,8 @@
 
         for s in range(blocks - 1, -1, -1):
             if s == 0:
+                if h > 0:
+                    early[...] += weight_term(1, h - 1)
 
                 @pl.when(c == 1)
                 def _():
@@ -274,7 +276,6 @@
             grad[0, h, pl.ds(s * reach, reach)] = (out * inverse).astype(BF16)
         edge_copy(h, 0).start()
         spread_grad(0, h)
-        spread_edge(0, h)
 
     def right_chain(h):
         left_feat[...] = feature(0, h)
@@ -372,9 +373,10 @@
 
         lay(depth + 1, i)
 
-    def give(side, goal, allowed, i):
+    def ready_part(side, goal, i):
         part_out[side, i] = gathered(i, goal).astype(BF16)
 
+    def give(side, allowed, i):
         @pl.when(allowed)
         def _():
             part_copy(side, i).start()
@@ -394,9 +396,7 @@
         left_chain(h)
         entering(h, 0)
         right_chain(h)
-        if h < depth - 1:
-            early[...] += weight_term(1, h)
-        else:
+        if h == depth - 1:
             for k in range(3):
                 lanes = pl.ds(k * 3 * cin, 3 * cin)
                 total = matmul(grad[1, h], patch[1, h, :, lanes], ((0,), (0,)))
@@ -409,10 +409,12 @@
                         pair_out[k, col, s % 2, s // 2] = piece.astype(BF16)
                 pair_copy(k).start()
         spread_grad(1, h)
+        spread_edge(0, h)
         spread_edge(1, h)
         if h == 0:
             for i in (0, 1):
-                give(0, -1, has_up, i)
+                ready_part(0, -1, i)
+                give(0, has_up, i)
             if rounds > 1:
                 hear_word(1)
             if rounds > 2:
@@ -450,7 +452,7 @@
 
     def put(goal):
         for i in (0, 1):
-            total = gathered(i, goal)
+            total = own_conv[i, goal, :, 0:cin]
             if goal == 0:
                 total = total + jnp.where(has_up, part_in[0, i].astype(F32), 0.0)
             if goal == depth - 1:
@@ -461,6 +463,11 @@
     def last_copy(k):
         return remote(whole.at[k, c], whole.at[k, c], whole_send.at[k], whole_recv.at[k], r, other)
 
+    for i in (0, 1):
+        ready_part(1, depth, i)
+        for goal in range(depth):
+            own_conv[i, goal, :, 0:cin] = gathered(i, goal)
+
     for k in range(3):
         cross_copy(k).wait_recv()
         total = acc[k, c, parity] + cross_in[k].astype(F32)
@@ -474,7 +481,7 @@
         lax.fori_loop(1, half, start_chunk, 0)
 
     for i in (0, 1):
-        give(1, depth, has_down, i)
+        give(1, has_down, i)
 
     @pl.when(has_down)
     def _():

time: 39 us -> 38.6 us (0.990)
  Pallas kernels: 38.2 us -> 37.8 us
where the time goes in v3:
time: 38.6 us; the launch traced here: 38.5 us
  Pallas kernels  37.8 us (98%)
  between operations  0.64 us (2%)
    pallas_call x1, Pallas kernels, on_device(): pl.pallas_call(functools.partial(kernel, rows, cols), out_shape=(jax.Shap...  36 us
    pallas_call x1, Pallas kernels, on_device(): pl.pallas_call(hand_over, out_shape=shapes, in_specs=[hbm] * 3, out_specs...  1.84 us

profile of v3, /device:TPU:16, one launch (start us, length us, event | category | flops | bytes accessed | tf_op | source)
XLA Modules:
  0.0 38.5 jit_solution(8995404875201880557)
XLA Ops:
  0.6 36.0 %stereo_backward.1 = (bf16[2,512,128]{2,1,0:T(8,128)(2,1)}, bf16[2,512,128]{2,1,0:T(8,128)(2,1)}, f32[32,1152]{1,0:T(8,128)}) custom-call(bf16[2,512,128]{2,1,0:T(8,128)(2,1)} %left_hbm.1, bf16[2,512,128]{2,1,0:T(8,128)(2,1)} %right_hbm.1, bf16[1152,256]{1,0:T(8,128)(2,1)} %weight_hbm.1, bf16[2,512,256]{2,1,0:T(8,128)(2,1)} %l0_hbm.1, ...), custom_call_target="tpu_custom_call" | custom-call | tf_op jit(solution)/shard_map/stereo_backward/pallas_call | solution.py:593
  36.6 1.8 %hand_over.1 = (bf16[2,512,128]{2,1,0:T(8,128)(2,1)}, bf16[2,512,128]{2,1,0:T(8,128)(2,1)}, f32[32,1152]{1,0:T(8,128)}) custom-call(bf16[2,512,128]{2,1,0:T(8,128)(2,1)} %get-tuple-element.6.a, bf16[2,512,128]{2,1,0:T(8,128)(2,1)} %get-tuple-element.7.b, f32[32,1152]{1,0:T(8,128)} %get-tuple-element.8.w), custom_call_target="tpu_custom_call" | custom-call | tf_op jit(solution)/shard_map/hand_over/pallas_call | solution.py:639

commit v4 on v3

--- a/solution.py
+++ b/solution.py
@@ -394,6 +394,10 @@
     for h in range(depth):
         entering(h, 1)
         left_chain(h)
+        if h == 0:
+            spread_edge(0, 0)
+            ready_part(0, -1, 0)
+            give(0, has_up, 0)
         entering(h, 0)
         right_chain(h)
         if h == depth - 1:
@@ -409,12 +413,12 @@
                         pair_out[k, col, s % 2, s // 2] = piece.astype(BF16)
                 pair_copy(k).start()
         spread_grad(1, h)
-        spread_edge(0, h)
+        if h > 0:
+            spread_edge(0, h)
         spread_edge(1, h)
         if h == 0:
-            for i in (0, 1):
-                ready_part(0, -1, i)
-                give(0, has_up, i)
+            ready_part(0, -1, 1)
+            give(0, has_up, 1)
             if rounds > 1:
                 hear_word(1)
             if rounds > 2:
@@ -479,9 +483,10 @@
             return carry
 
         lax.fori_loop(1, half, start_chunk, 0)
-
-    for i in (0, 1):
-        give(1, has_down, i)
+        if k == 1:
+            give(1, has_down, 0)
+            give(1, has_down, 1)
+
 
     @pl.when(has_down)
     def _():

time: 38.6 us -> 38.2 us (0.990); the launches traced: 38.5 us -> 37.6 us
  Pallas kernels: 37.8 us -> 37 us
    pallas_call x1, Pallas kernels: 36 us -> 35.1 us  [on_device(): pl.pallas_call(functools.partial(kernel, rows, cols), out_shape=(jax.Shap...]
where the time goes in v4:
time: 38.2 us; the launch traced here: 37.6 us
  Pallas kernels  37 us (97%)
  between operations  0.64 us (2%)
    pallas_call x1, Pallas kernels, on_device(): pl.pallas_call(functools.partial(kernel, rows, cols), out_shape=(jax.Shap...  35.1 us
    pallas_call x1, Pallas kernels, on_device(): pl.pallas_call(hand_over, out_shape=shapes, in_specs=[hbm] * 3, out_specs...  1.84 us

profile of v4, /device:TPU:16, one launch (start us, length us, event | category | flops | bytes accessed | tf_op | source)
XLA Modules:
  0.0 37.6 jit_solution(8703363230965155819)
XLA Ops:
  0.6 35.1 %stereo_backward.1 = (bf16[2,512,128]{2,1,0:T(8,128)(2,1)}, bf16[2,512,128]{2,1,0:T(8,128)(2,1)}, f32[32,1152]{1,0:T(8,128)}) custom-call(bf16[2,512,128]{2,1,0:T(8,128)(2,1)} %left_hbm.1, bf16[2,512,128]{2,1,0:T(8,128)(2,1)} %right_hbm.1, bf16[1152,256]{1,0:T(8,128)(2,1)} %weight_hbm.1, bf16[2,512,256]{2,1,0:T(8,128)(2,1)} %l0_hbm.1, ...), custom_call_target="tpu_custom_call" | custom-call | tf_op jit(solution)/shard_map/stereo_backward/pallas_call | solution.py:598
  35.8 1.8 %hand_over.1 = (bf16[2,512,128]{2,1,0:T(8,128)(2,1)}, bf16[2,512,128]{2,1,0:T(8,128)(2,1)}, f32[32,1152]{1,0:T(8,128)}) custom-call(bf16[2,512,128]{2,1,0:T(8,128)(2,1)} %get-tuple-element.6.a, bf16[2,512,128]{2,1,0:T(8,128)(2,1)} %get-tuple-element.7.b, f32[32,1152]{1,0:T(8,128)} %get-tuple-element.8.w), custom_call_target="tpu_custom_call" | custom-call | tf_op jit(solution)/shard_map/hand_over/pallas_call | solution.py:644

commit v5 on v4

--- a/solution.py
+++ b/solution.py
@@ -483,9 +483,8 @@
             return carry
 
         lax.fori_loop(1, half, start_chunk, 0)
-        if k == 1:
-            give(1, has_down, 0)
-            give(1, has_down, 1)
+        if k > 0:
+            give(1, has_down, k - 1)
 
 
     @pl.when(has_down)

time: 38.2 us -> 38 us (level); the launches traced: 37.6 us -> 37.9 us
  no operation moved by 1% of the time
where the time goes in v5:
time: 38 us; the launch traced here: 37.9 us
  Pallas kernels  37.2 us (98%)
  between operations  0.64 us (2%)
    pallas_call x1, Pallas kernels, on_device(): pl.pallas_call(functools.partial(kernel, rows, cols), out_shape=(jax.Shap...  35.4 us
    pallas_call x1, Pallas kernels, on_device(): pl.pallas_call(hand_over, out_shape=shapes, in_specs=[hbm] * 3, out_specs...  1.84 us

profile of v5, /device:TPU:16, one launch (start us, length us, event | category | flops | bytes accessed | tf_op | source)
XLA Modules:
  0.0 37.9 jit_solution(14210919444261990459)
XLA Ops:
  0.6 35.4 %stereo_backward.1 = (bf16[2,512,128]{2,1,0:T(8,128)(2,1)}, bf16[2,512,128]{2,1,0:T(8,128)(2,1)}, f32[32,1152]{1,0:T(8,128)}) custom-call(bf16[2,512,128]{2,1,0:T(8,128)(2,1)} %left_hbm.1, bf16[2,512,128]{2,1,0:T(8,128)(2,1)} %right_hbm.1, bf16[1152,256]{1,0:T(8,128)(2,1)} %weight_hbm.1, bf16[2,512,256]{2,1,0:T(8,128)(2,1)} %l0_hbm.1, ...), custom_call_target="tpu_custom_call" | custom-call | tf_op jit(solution)/shard_map/stereo_backward/pallas_call | solution.py:597
  36.0 1.8 %hand_over.1 = (bf16[2,512,128]{2,1,0:T(8,128)(2,1)}, bf16[2,512,128]{2,1,0:T(8,128)(2,1)}, f32[32,1152]{1,0:T(8,128)}) custom-call(bf16[2,512,128]{2,1,0:T(8,128)(2,1)} %get-tuple-element.6.a, bf16[2,512,128]{2,1,0:T(8,128)(2,1)} %get-tuple-element.7.b, f32[32,1152]{1,0:T(8,128)} %get-tuple-element.8.w), custom_call_target="tpu_custom_call" | custom-call | tf_op jit(solution)/shard_map/hand_over/pallas_call | solution.py:643

commit v6 on v4

--- a/solution.py
+++ b/solution.py
@@ -485,7 +485,6 @@
         lax.fori_loop(1, half, start_chunk, 0)
         if k == 1:
             give(1, has_down, 0)
-            give(1, has_down, 1)
 
 
     @pl.when(has_down)
@@ -508,6 +507,8 @@
         lax.fori_loop(1, half, wait_chunk, 0)
         whole[k, c] = lax.fori_loop(1, half, add_chunk, acc[k, c, parity, place_in_half])
         last_copy(k).start()
+        if k == 0:
+            give(1, has_down, 1)
 
     @pl.when(has_up)
     def _():

time: 38.2 us -> 38 us (level); the launches traced: 37.6 us -> 37.9 us
  no operation moved by 1% of the time
where the time goes in v6:
time: 38 us; the launch traced here: 37.9 us
  Pallas kernels  37.2 us (98%)
  between operations  0.64 us (2%)
    pallas_call x1, Pallas kernels, on_device(): pl.pallas_call(functools.partial(kernel, rows, cols), out_shape=(jax.Shap...  35.4 us
    pallas_call x1, Pallas kernels, on_device(): pl.pallas_call(hand_over, out_shape=shapes, in_specs=[hbm] * 3, out_specs...  1.84 us

profile of v6, /device:TPU:16, one launch (start us, length us, event | category | flops | bytes accessed | tf_op | source)
XLA Modules:
  0.0 37.9 jit_solution(13589060911773314543)
XLA Ops:
  0.6 35.4 %stereo_backward.1 = (bf16[2,512,128]{2,1,0:T(8,128)(2,1)}, bf16[2,512,128]{2,1,0:T(8,128)(2,1)}, f32[32,1152]{1,0:T(8,128)}) custom-call(bf16[2,512,128]{2,1,0:T(8,128)(2,1)} %left_hbm.1, bf16[2,512,128]{2,1,0:T(8,128)(2,1)} %right_hbm.1, bf16[1152,256]{1,0:T(8,128)(2,1)} %weight_hbm.1, bf16[2,512,256]{2,1,0:T(8,128)(2,1)} %l0_hbm.1, ...), custom_call_target="tpu_custom_call" | custom-call | tf_op jit(solution)/shard_map/stereo_backward/pallas_call | solution.py:599
  36.0 1.8 %hand_over.1 = (bf16[2,512,128]{2,1,0:T(8,128)(2,1)}, bf16[2,512,128]{2,1,0:T(8,128)(2,1)}, f32[32,1152]{1,0:T(8,128)}) custom-call(bf16[2,512,128]{2,1,0:T(8,128)(2,1)} %get-tuple-element.6.a, bf16[2,512,128]{2,1,0:T(8,128)(2,1)} %get-tuple-element.7.b, f32[32,1152]{1,0:T(8,128)} %get-tuple-element.8.w), custom_call_target="tpu_custom_call" | custom-call | tf_op jit(solution)/shard_map/hand_over/pallas_call | solution.py:645
